TPU v7x, 512 devices: a whole 4x8x8 slice. The times are simulated.
512 devices in a mesh: wide: 128 (over y, z, core), rep: 4 (over x).
Axes of the slice: x: 4, y: 8, z: 8, core: 2. Of those that a mesh axis runs over, the one named last changes fastest.
Arguments:
- node_feats: bfloat16 [131072, 512], P('wide'), may hold values from -6 to 6
- w_self: bfloat16 [512, 512], replicated, may hold values from -0.25 to 0.25
- w_neigh: bfloat16 [512, 512], replicated, may hold values from -0.25 to 0.25
- send_rows: int32 [128, 128, 32], P('wide', None, 'rep'), may hold values from 0 to 1023
- tile_dst: int32 [128, 4, 128], P('wide', 'rep'), may hold values from 0 to 15
- tile_src: int32 [128, 4, 128], P('wide', 'rep'), may hold values from 0 to 31
- tile_bits: int32 [128, 4, 32768], P('wide', 'rep'), may hold values from 0 to 65280
- norm_count: int32 [131072], P('wide'), may hold values from 512 to 2048
- grad_out: bfloat16 [131072, 512], P(('wide', 'rep')), may hold values from -6 to 6
Outputs:
- out_feats: bfloat16 [131072, 512], P(('wide', 'rep'))
- grad_feats: bfloat16 [131072, 512], P(('wide', 'rep'))
- grad_self: bfloat16 [512, 512], replicated
- grad_neigh: bfloat16 [512, 512], replicated
All inputs are finite; a program needn't handle non-finite values.
Results may differ from a plain program's by a relative error of at most 0.014.
Values may be sent and summed in bfloat16 or wider, within the bound.
No kernel may reach another device: no remote copies, remote signals or barrier semaphores. Data moves between devices by JAX's collectives and lax.ppermute only.
A program may use at most 64 MiB of HBM per device.

v0:
```python
import math
import jax
import jax.numpy as jnp
from jax import lax
from jax.sharding import PartitionSpec as P

BLOCK = 64


def unpack_bits(packed, tile_count, block_size):
    shaped = packed.reshape(tile_count, block_size, block_size // 16)
    shift_list = jnp.arange(16, dtype=jnp.int32)
    bit_grid = jnp.bitwise_and(jnp.right_shift(shaped[..., None], shift_list), 1)
    return bit_grid.reshape(tile_count, block_size, block_size)


def times_transposed(left, right):
    return lax.dot_general(
        left, right, (((1,), (1,)), ((), ())), preferred_element_type=jnp.float32
    )


def on_device(
    node_feats, w_self, w_neigh, send_rows, tile_dst, tile_src, tile_bits, norm_count, grad_out
):
    node_rows, feat_width = node_feats.shape
    peer_count = lax.axis_size("wide")
    replicas = lax.axis_size("rep")
    slot_count = send_rows.shape[2]
    tile_total = tile_dst.shape[2]
    block_size = BLOCK
    quarter = node_rows // replicas
    rep_index = lax.axis_index("rep")
    dst_count = node_rows // block_size
    group_size = math.gcd(tile_total, 32)
    send_index = send_rows[0]
    outgoing = jnp.take(node_feats, send_index.reshape(-1), axis=0).reshape(
        peer_count, slot_count, feat_width
    )
    incoming = lax.all_to_all(outgoing, "wide", split_axis=0, concat_axis=0, tiled=True)
    src_table = jnp.concatenate(
        [node_feats, incoming.reshape(peer_count * slot_count, feat_width)], axis=0
    )
    source_blocks = src_table.reshape(-1, block_size, feat_width)
    src_count = source_blocks.shape[0]
    tile_masks = unpack_bits(tile_bits[0, 0], tile_total, block_size).astype(jnp.bfloat16)
    grouped_masks = tile_masks.reshape(-1, group_size, block_size, block_size)
    grouped_dst = tile_dst[0, 0].reshape(-1, group_size)
    grouped_src = tile_src[0, 0].reshape(-1, group_size)

    def forward_group(running, group_items):
        mask_part, dst_part, src_part = group_items
        picked = jnp.take(source_blocks, src_part, axis=0)
        products = jnp.einsum("tij,tjf->tif", mask_part, picked, preferred_element_type=jnp.float32)
        return (running.at[dst_part].add(products), None)

    partial_sum, _ = lax.scan(
        forward_group,
        jnp.zeros((dst_count, block_size, feat_width), jnp.float32),
        (grouped_masks, grouped_dst, grouped_src),
    )
    partial_sum = partial_sum.reshape(node_rows, feat_width)
    summed = lax.psum(partial_sum, "rep")
    own_sums = lax.dynamic_slice_in_dim(summed, rep_index * quarter, quarter, 0)
    scale_all = lax.rsqrt(norm_count.astype(jnp.float32))
    own_scale = lax.dynamic_slice_in_dim(scale_all, rep_index * quarter, quarter, 0)
    own_feats = lax.dynamic_slice_in_dim(node_feats, rep_index * quarter, quarter, 0)
    own_agg = (own_sums * own_scale[:, None]).astype(jnp.bfloat16)
    pre_act = jnp.dot(own_feats, w_self, preferred_element_type=jnp.float32) + jnp.dot(
        own_agg, w_neigh, preferred_element_type=jnp.float32
    )
    sigmoid = jax.nn.sigmoid(pre_act)
    out_feats = (pre_act * sigmoid).astype(jnp.bfloat16)
    grad_pre = (grad_out.astype(jnp.float32) * sigmoid * (1.0 + pre_act * (1.0 - sigmoid))).astype(
        jnp.bfloat16
    )
    dims_rows = (((0,), (0,)), ((), ()))
    self_term = lax.dot_general(own_feats, grad_pre, dims_rows, preferred_element_type=jnp.float32)
    neigh_term = lax.dot_general(own_agg, grad_pre, dims_rows, preferred_element_type=jnp.float32)
    summed_self, summed_neigh = lax.psum((self_term, neigh_term), ("wide", "rep"))
    own_grad_agg = (times_transposed(grad_pre, w_neigh) * own_scale[:, None]).astype(jnp.bfloat16)
    grad_agg = lax.all_gather(own_grad_agg, "rep", axis=0, tiled=True)
    agg_blocks = grad_agg.reshape(dst_count, block_size, feat_width)

    def backward_group(running, group_items):
        mask_part, dst_part, src_part = group_items
        picked = jnp.take(agg_blocks, dst_part, axis=0)
        products = jnp.einsum("tij,tif->tjf", mask_part, picked, preferred_element_type=jnp.float32)
        return (running.at[src_part].add(products), None)

    table_grad, _ = lax.scan(
        backward_group,
        jnp.zeros((src_count, block_size, feat_width), jnp.float32),
        (grouped_masks, grouped_dst, grouped_src),
    )
    table_grad = table_grad.reshape(src_count * block_size, feat_width)
    local_grad = table_grad[:node_rows]
    halo_grad = (
        table_grad[node_rows:].astype(jnp.bfloat16).reshape(peer_count, slot_count, feat_width)
    )
    returned = lax.all_to_all(halo_grad, "wide", split_axis=0, concat_axis=0, tiled=True)
    returned_rows = (
        jnp.zeros((node_rows, feat_width), jnp.float32)
        .at[send_index.reshape(-1)]
        .add(returned.reshape(-1, feat_width).astype(jnp.float32))
    )
    own_total = lax.psum_scatter(
        (local_grad + returned_rows).astype(jnp.bfloat16), "rep", scatter_dimension=0, tiled=True
    ).astype(jnp.float32)
    grad_feats = (own_total + times_transposed(grad_pre, w_self)).astype(jnp.bfloat16)
    return (
        out_feats,
        grad_feats,
        summed_self.astype(jnp.bfloat16),
        summed_neigh.astype(jnp.bfloat16),
    )


def solution(mesh):
    in_specs = (
        P("wide", None),
        P(),
        P(),
        P("wide", None, "rep"),
        P("wide", "rep", None),
        P("wide", "rep", None),
        P("wide", "rep", None),
        P("wide"),
        P(("wide", "rep"), None),
    )
    out_specs = (P(("wide", "rep"), None), P(("wide", "rep"), None), P(), P())
    return jax.shard_map(
        on_device, mesh=mesh, in_specs=in_specs, out_specs=out_specs, check_vma=False
    )
```

profile of v0, /device:TPU:1, one launch (start us, length us, event | category | flops | bytes accessed | tf_op | source)
XLA Modules:
  0.0 459.9 jit_solution(16109861953868291241)
XLA Ops:
  7.2 0.8 compare_and_fusion.2
  7.9 0.8 copy.18
  8.7 0.1 copy.17
  8.8 0.1 reshape_squeeze.15
  9.0 5.4 %gather_fusion.2 = bf16[1024,512]{1,0:T(8,128)(2,1)S(1)} fusion(bf16[1024,512]{1,0:T(8,128)(2,1)} %param.13, s32[1024]{0:T(1024)S(1)} %broadcast_clamp_fusion), kind=kCustom, calls=%fused_computation.2 | custom fusion | bytes 2101248 | tf_op jit(solution)/shard_map/jit(_take)/gather | solution.py:37
  14.4 1.2 bitcast_select_fusion
  15.5 18.4 %all-to-all-start = ((bf16[128,8,512]{2,1,0:T(8,128)(2,1)}), bf16[128,8,512]{2,1,0:T(8,128)(2,1)S(1)}, u32[]{:S(2)}, u32[]{:S(2)}) async-start(bf16[128,8,512]{2,1,0:T(8,128)(2,1)} %bitcast_select_fusion), calls=%async_computation | async-start | bytes 2097152 | tf_op jit(solution)/shard_map/all_to_all | solution.py:40
  34.0 0.5 broadcast.165
  34.5 0.7 reduce.9
  35.2 0.7 reduce.11
  35.9 0.1 reshape_squeeze.13
  36.0 0.1 shift_right_arithmetic.27
  36.1 1.0 reduce.10
  37.1 5.7 %shift_right_arithmetic.23 = s32[128,64,4]{2,1,0:T(8,128)} reshape(s32[32768]{0:T(1024)S(1)} %reduce.10) | data formatting | bytes 262144 | tf_op jit(solution)/shard_map/shift_right_arithmetic | solution.py:13
  42.7 3.0 copy.16
  45.7 0.3 shift_right_arithmetic.24
  46.1 2.1 and_convert_fusion
  48.2 16.2 %all-to-all-done = bf16[128,8,512]{2,1,0:T(8,128)(2,1)S(1)} async-done(((bf16[128,8,512]{2,1,0:T(8,128)(2,1)}), bf16[128,8,512]{2,1,0:T(8,128)(2,1)S(1)}, u32[]{:S(2)}, u32[]{:S(2)}) %all-to-all-start) | async-done | bytes 1048608 | tf_op jit(solution)/shard_map/all_to_all | solution.py:40
  64.4 1.5 pad_maximum_fusion
  65.9 0.2 broadcast_in_dim.43
  66.1 58.5 %while.20 = (s32[]{:T(128)}, f32[16,64,512]{2,1,0:T(8,128)S(1)}, s32[4,32]{1,0:T(4,128)S(1)}, bf16[4,32,64,64]{2,3,1,0:T(8,128)(2,1)}, s32[4,32]{1,0:T(4,128)S(1)}, /*index=5*/bf16[32,64,512]{2,1,0:T(8,128)(2,1)}, s32[]{:T(128)}) while((s32[]{:T(128)}, f32[16,64,512]{2,1,0:T(8,128)S(1)}, s32[4,32]{1,0:T(4,128)S(1)}, ...), condition=%wide.region_2.3_spmd, body=%wide.region_0.0_spmd.sunk | while | flops 136316288 | bytes 23598240 | solution.py:57
  66.2 3.6 gather_fusion
  69.8 4.5 fusion.53
  74.3 6.5 %scatter_fusion = f32[16,64,512]{2,1,0:T(8,128)S(1)} fusion(f32[16,64,512]{2,1,0:T(8,128)S(1)} %get-tuple-element.204, s32[32]{0:T(128)S(1)} %get-tuple-element.186, f32[32,64,512]{2,1,0:T(8,128)} %fusion.53), kind=kCustom, calls=%fused_computation.3.clone.1 | custom fusion | flops 1048576 | bytes 12583040 | tf_op jit(solution)/shard_map/while/body/eval_jaxpr/scatter-add | solution.py:55
  80.8 3.6 gather_fusion
  84.4 4.5 fusion.53
  88.9 6.5 %scatter_fusion = f32[16,64,512]{2,1,0:T(8,128)S(1)} fusion(f32[16,64,512]{2,1,0:T(8,128)S(1)} %get-tuple-element.204, s32[32]{0:T(128)S(1)} %get-tuple-element.186, f32[32,64,512]{2,1,0:T(8,128)} %fusion.53), kind=kCustom, calls=%fused_computation.3.clone.1 | custom fusion | flops 1048576 | bytes 12583040 | tf_op jit(solution)/shard_map/while/body/eval_jaxpr/scatter-add | solution.py:55
  95.4 3.6 gather_fusion
  99.1 4.5 fusion.53
  103.5 6.5 %scatter_fusion = f32[16,64,512]{2,1,0:T(8,128)S(1)} fusion(f32[16,64,512]{2,1,0:T(8,128)S(1)} %get-tuple-element.204, s32[32]{0:T(128)S(1)} %get-tuple-element.186, f32[32,64,512]{2,1,0:T(8,128)} %fusion.53), kind=kCustom, calls=%fused_computation.3.clone.1 | custom fusion | flops 1048576 | bytes 12583040 | tf_op jit(solution)/shard_map/while/body/eval_jaxpr/scatter-add | solution.py:55
  110.1 3.6 gather_fusion
  113.7 4.5 fusion.53
  118.2 6.5 %scatter_fusion = f32[16,64,512]{2,1,0:T(8,128)S(1)} fusion(f32[16,64,512]{2,1,0:T(8,128)S(1)} %get-tuple-element.204, s32[32]{0:T(128)S(1)} %get-tuple-element.186, f32[32,64,512]{2,1,0:T(8,128)} %fusion.53), kind=kCustom, calls=%fused_computation.3.clone.1 | custom fusion | flops 1048576 | bytes 12583040 | tf_op jit(solution)/shard_map/while/body/eval_jaxpr/scatter-add | solution.py:55
  124.7 1.3 copy-done.1
  126.0 0.2 all-gather.2.cloned.1.call-start
  126.4 1.2 fusion.29
  127.6 62.0 %all-reduce.4.cloned.1.call-done = f32[1024,512]{1,0:T(8,128)} async-done(((f32[1024,512]{1,0:T(8,128)}), f32[1024,512]{1,0:T(8,128)}) %all-reduce.4.cloned.1.call-update) | async-done | bytes 2097168 | tf_op jit(solution)/shard_map/psum | solution.py:63
  189.6 2.3 multiply_convert_fusion
  192.0 1.0 fusion.24
  193.0 28.4 %all-gather.2.cloned.1.call-done = bf16[1024,512]{1,0:T(8,128)(2,1)} async-done(((bf16[256,512]{1,0:T(8,128)(2,1)}), bf16[1024,512]{1,0:T(8,128)(2,1)}) %all-gather.2.cloned.1.call-update) | async-done | bytes 1048592 | tf_op jit(solution)/shard_map/all_gather | solution.py:82
  221.4 2.5 broadcast_in_dim.46
  223.9 62.5 %while.21 = (s32[]{:T(128)}, f32[32,64,512]{2,1,0:T(8,128)}, s32[4,32]{1,0:T(4,128)S(1)}, bf16[4,32,64,64]{2,3,1,0:T(8,128)(2,1)}, s32[4,32]{1,0:T(4,128)S(1)}, /*index=5*/bf16[16,64,512]{2,1,0:T(8,128)(2,1)}, s32[]{:T(128)}) while((s32[]{:T(128)}, f32[32,64,512]{2,1,0:T(8,128)}, s32[4,32]{1,0:T(4,128)S(1)}, ...), condition=%wide.region_6.7_spmd, body=%wide.region_4.6_spmd.sunk | while | flops 136316288 | bytes 23598240 | solution.py:91
  224.0 1.9 gather_fusion.1
  225.9 3.8 fusion.57
  229.7 9.8 %scatter_fusion.1 = f32[32,64,512]{2,1,0:T(8,128)} fusion(f32[32,64,512]{2,1,0:T(8,128)} %get-tuple-element.225, s32[32]{0:T(128)S(1)} %get-tuple-element.194, f32[32,64,512]{2,1,0:T(8,128)} %fusion.57), kind=kCustom, calls=%fused_computation.4.clone.1 | custom fusion | flops 1048576 | bytes 12583040 | tf_op jit(solution)/shard_map/while/body/eval_jaxpr/scatter-add | solution.py:89
  239.5 1.9 gather_fusion.1
  241.4 3.7 fusion.57
  245.1 9.8 %scatter_fusion.1 = f32[32,64,512]{2,1,0:T(8,128)} fusion(f32[32,64,512]{2,1,0:T(8,128)} %get-tuple-element.225, s32[32]{0:T(128)S(1)} %get-tuple-element.194, f32[32,64,512]{2,1,0:T(8,128)} %fusion.57), kind=kCustom, calls=%fused_computation.4.clone.1 | custom fusion | flops 1048576 | bytes 12583040 | tf_op jit(solution)/shard_map/while/body/eval_jaxpr/scatter-add | solution.py:89
  255.0 1.9 gather_fusion.1
  256.9 3.7 fusion.57
  260.6 10.0 %scatter_fusion.1 = f32[32,64,512]{2,1,0:T(8,128)} fusion(f32[32,64,512]{2,1,0:T(8,128)} %get-tuple-element.225, s32[32]{0:T(128)S(1)} %get-tuple-element.194, f32[32,64,512]{2,1,0:T(8,128)} %fusion.57), kind=kCustom, calls=%fused_computation.4.clone.1 | custom fusion | flops 1048576 | bytes 12583040 | tf_op jit(solution)/shard_map/while/body/eval_jaxpr/scatter-add | solution.py:89
  270.7 1.9 gather_fusion.1
  272.6 3.7 fusion.57
  276.3 10.1 %scatter_fusion.1 = f32[32,64,512]{2,1,0:T(8,128)} fusion(f32[32,64,512]{2,1,0:T(8,128)} %get-tuple-element.225, s32[32]{0:T(128)S(1)} %get-tuple-element.194, f32[32,64,512]{2,1,0:T(8,128)} %fusion.57), kind=kCustom, calls=%fused_computation.4.clone.1 | custom fusion | flops 1048576 | bytes 12583040 | tf_op jit(solution)/shard_map/while/body/eval_jaxpr/scatter-add | solution.py:89
  286.4 2.8 slice.22
  289.2 15.9 %all-to-all-start.1 = ((bf16[128,8,512]{2,1,0:T(8,128)(2,1)}), bf16[128,8,512]{2,1,0:T(8,128)(2,1)}, u32[]{:S(2)}, u32[]{:S(2)}) async-start(bf16[128,8,512]{2,1,0:T(8,128)(2,1)} %bitcast.21), calls=%async_computation.1 | async-start | bytes 2097152 | tf_op jit(solution)/shard_map/all_to_all | solution.py:101
  305.1 1.9 slice.11
  307.0 28.2 %all-to-all-done.1 = bf16[128,8,512]{2,1,0:T(8,128)(2,1)} async-done(((bf16[128,8,512]{2,1,0:T(8,128)(2,1)}), bf16[128,8,512]{2,1,0:T(8,128)(2,1)}, u32[]{:S(2)}, u32[]{:S(2)}) %all-to-all-start.1) | async-done | bytes 1048608 | tf_op jit(solution)/shard_map/all_to_all | solution.py:101
  335.2 8.0 %scatter_custom_fusion.2 = f32[1024,512]{1,0:T(8,128)S(1)} fusion(f32[1024,512]{1,0:T(8,128)S(1)} %bitcast.83, s32[1024]{0:T(1024)S(1)} %bitcast.86, bf16[128,8,512]{2,1,0:T(8,128)(2,1)} %all-to-all-done.1), kind=kCustom, calls=%fused_computation.45 | custom fusion | flops 1048576 | bytes 3145728 | tf_op jit(solution)/shard_map/scatter-add | solution.py:105
  343.2 1.1 convert_element_type.58
  344.3 1.5 fusion.33
  345.8 1.3 fusion.27
  347.0 104.4 %all-reduce.5 = (bf16[512,512]{1,0:T(8,128)(2,1)}, bf16[512,512]{1,0:T(8,128)(2,1)}) all-reduce(f32[512,512]{1,0:T(8,128)S(1)} %fusion.27, f32[512,512]{1,0:T(8,128)S(1)} %fusion.33), channel_id=1, replica_groups=mesh['wide'=128,'rep'=4] {'wide','rep'}, use_global_device_ids=true, to_apply=%region_9.10 | all-reduce | flops 524288 | bytes 3145728 | tf_op jit(solution)/shard_map/psum | solution.py:80
  451.4 2.0 fusion.25
  (51 shorter events, 0.6 us)
Async XLA Ops:
  7.2 182.5 %copy-start = (bf16[512,512]{1,0:T(8,128)(2,1)S(1)}, bf16[512,512]{1,0:T(8,128)(2,1)}, u32[]{:S(2)}) copy-start(bf16[512,512]{1,0:T(8,128)(2,1)} %param.15) | copy-start | bytes 1572868
  14.3 20.2 %copy-start.6 = (s32[1,1,128]{2,1,0:T(1,128)S(1)}, s32[1,1,128]{2,1,0:T(1,128)}, u32[]{:S(2)}) copy-start(s32[1,1,128]{2,1,0:T(1,128)} %param.17) | copy-start | bytes 1540
  14.3 20.9 %copy-start.7 = (s32[1,1,128]{2,1,0:T(1,128)S(1)}, s32[1,1,128]{2,1,0:T(1,128)}, u32[]{:S(2)}) copy-start(s32[1,1,128]{2,1,0:T(1,128)} %param.18) | copy-start | bytes 1540
  14.4 21.8 %copy-start.4 = (s32[1,1,32768]{2,1,0:T(1,128)S(1)}, s32[1,1,32768]{2,1,0:T(1,128)}, u32[]{:S(2)}) copy-start(s32[1,1,32768]{2,1,0:T(1,128)} %param.19) | copy-start | bytes 393220
  15.5 48.9 %all-to-all-start = ((bf16[128,8,512]{2,1,0:T(8,128)(2,1)}), bf16[128,8,512]{2,1,0:T(8,128)(2,1)S(1)}, u32[]{:S(2)}, u32[]{:S(2)}) async-start(bf16[128,8,512]{2,1,0:T(8,128)(2,1)} %bitcast_select_fusion), calls=%async_computation | async-start | bytes 2097152 | tf_op jit(solution)/shard_map/all_to_all | solution.py:40
  34.0 155.7 %all-reduce.4.cloned.1.call-start = ((), (), s32[]{:S(2)}) async-start(), calls=%async_computation.3 | async-start | bytes 4194304 | tf_op jit(solution)/shard_map/psum | solution.py:63
  46.1 18.3 %copy-start.2 = (bf16[1024,512]{1,0:T(8,128)(2,1)S(1)}, bf16[1024,512]{1,0:T(8,128)(2,1)}, u32[]{:S(2)}) copy-start(bf16[1024,512]{1,0:T(8,128)(2,1)} %param.13) | copy-start | bytes 3145732
  124.7 1.3 copy-start.1
  124.7 1.6 copy-start.5
  124.7 1.7 copy-start.3
  126.0 95.4 %all-gather.2.cloned.1.call-start = ((), (), s32[]{:S(2)}) async-start(), calls=%async_computation.4 | async-start | bytes 1310720 | tf_op jit(solution)/shard_map/all_gather | solution.py:82
  289.2 46.0 %all-to-all-start.1 = ((bf16[128,8,512]{2,1,0:T(8,128)(2,1)}), bf16[128,8,512]{2,1,0:T(8,128)(2,1)}, u32[]{:S(2)}, u32[]{:S(2)}) async-start(bf16[128,8,512]{2,1,0:T(8,128)(2,1)} %bitcast.21), calls=%async_computation.1 | async-start | bytes 2097152 | tf_op jit(solution)/shard_map/all_to_all | solution.py:101
  305.1 146.3 %reduce-scatter.2.cloned.1.call-start = ((), (), s32[]{:S(2)}) async-start(), calls=%async_computation.5 | async-start | bytes 1310720 | tf_op jit(solution)/shard_map/reduce_scatter | solution.py:107
Sparse Core Ops, SparseCore 0:
  126.2 63.4 all-reduce.3
  193.2 28.2 all-gather.1
  344.4 20.2 reduce-scatter.1
where the time goes:
time: 462 us; the launch traced here: 460 us
  waiting for transfers between devices  135 us (29%)
  blocking collectives  104 us (23%)
  other arithmetic  82.7 us (18%)
  local copies, waits for them, and re-layouts  47 us (10%)
  matrix products  42.2 us (9%)
  starting transfers between devices  34.6 us (7%)
  between operations  14 us (3%)
    psum x1, blocking collectives, on_device(): lax.psum((self_term, neigh_term), ('wide', 'rep'))  104 us
    psum x1, waiting for transfers between devices, on_device(): summed = lax.psum(partial_sum, 'rep')  62 us
    scatter-add x4, other arithmetic, backward_group(): return (running.at[src_part].add(products), None)  39.6 us
    all_gather x1, waiting for transfers between devices, on_device(): grad_agg = lax.all_gather(own_grad_agg, 'rep', axis=0, tiled=True)  28.4 us
    all_to_all x1, waiting for transfers between devices, on_device(): lax.all_to_all(halo_grad, 'wide', split_axis=0, concat_axis=0, tiled=True)  28.2 us
    scatter-add x4, other arithmetic, forward_group(): return (running.at[dst_part].add(products), None)  25.9 us
    all_to_all x1, starting transfers between devices, on_device(): lax.all_to_all(outgoing, 'wide', split_axis=0, concat_axis=0, tiled=True)  18.4 us
    dot_general x4, matrix products, forward_group(): jnp.einsum('tij,tjf->tif', mask_part, picked, preferred_element_type=jnp....  17.9 us
  transfers between devices with their start and end apart: 5, of which 4 were waited for; matrix products, arithmetic and copies ran while one was open for 4% of the time, Pallas kernels for 0%

commit v1 on v0

--- a/solution.py
+++ b/solution.py
@@ -60,7 +60,7 @@
         (grouped_masks, grouped_dst, grouped_src),
     )
     partial_sum = partial_sum.reshape(node_rows, feat_width)
-    summed = lax.psum(partial_sum, "rep")
+    summed = jnp.sum(lax.all_gather(partial_sum, "rep"), axis=0)
     own_sums = lax.dynamic_slice_in_dim(summed, rep_index * quarter, quarter, 0)
     scale_all = lax.rsqrt(norm_count.astype(jnp.float32))
     own_scale = lax.dynamic_slice_in_dim(scale_all, rep_index * quarter, quarter, 0)

time: 462 us -> 487 us (1.054)
  waiting for transfers between devices: 135 us -> 154 us
    all_gather x0 -> x1, waiting for transfers between devices: none -> 80.2 us  [on_device(): summed = jnp.sum(lax.all_gather(partial_sum, 'rep'), axis=0)]
    psum x1 -> x0, waiting for transfers between devices: 62 us -> none  [on_device(): summed = lax.psum(partial_sum, 'rep')]
where the time goes in v1:
time: 487 us; the launch traced here: 485 us
  waiting for transfers between devices  154 us (32%)
  blocking collectives  104 us (21%)
  other arithmetic  87.2 us (18%)
  local copies, waits for them, and re-layouts  46.8 us (10%)
  matrix products  43.6 us (9%)
  starting transfers between devices  34.6 us (7%)
  between operations  14 us (3%)
    psum x1, blocking collectives, on_device(): lax.psum((self_term, neigh_term), ('wide', 'rep'))  104 us
    all_gather x1, waiting for transfers between devices, on_device(): summed = jnp.sum(lax.all_gather(partial_sum, 'rep'), axis=0)  80.2 us
    scatter-add x4, other arithmetic, backward_group(): return (running.at[src_part].add(products), None)  39.5 us
    all_gather x1, waiting for transfers between devices, on_device(): grad_agg = lax.all_gather(own_grad_agg, 'rep', axis=0, tiled=True)  29.6 us
    all_to_all x1, waiting for transfers between devices, on_device(): lax.all_to_all(halo_grad, 'wide', split_axis=0, concat_axis=0, tiled=True)  28.2 us
    scatter-add x4, other arithmetic, forward_group(): return (running.at[dst_part].add(products), None)  25.9 us
    all_to_all x1, starting transfers between devices, on_device(): lax.all_to_all(outgoing, 'wide', split_axis=0, concat_axis=0, tiled=True)  18.4 us
    dot_general x4, matrix products, forward_group(): jnp.einsum('tij,tjf->tif', mask_part, picked, preferred_element_type=jnp....  17.8 us
  transfers between devices with their start and end apart: 5, of which 4 were waited for; matrix products, arithmetic and copies ran while one was open for 4% of the time, Pallas kernels for 0%

profile of v1, /device:TPU:1, one launch (start us, length us, event | category | flops | bytes accessed | tf_op | source)
XLA Modules:
  0.0 485.1 jit_solution(8249489644476091721)
XLA Ops:
  7.2 0.8 compare_and_fusion.2
  7.9 0.8 copy.22
  8.7 0.1 copy.21
  8.8 0.1 reshape_squeeze.15
  9.0 5.4 %gather_fusion.2 = bf16[1024,512]{1,0:T(8,128)(2,1)S(1)} fusion(bf16[1024,512]{1,0:T(8,128)(2,1)} %param.13, s32[1024]{0:T(1024)S(1)} %broadcast_clamp_fusion), kind=kCustom, calls=%fused_computation.2 | custom fusion | bytes 2101248 | tf_op jit(solution)/shard_map/jit(_take)/gather | solution.py:37
  14.4 1.2 bitcast_select_fusion
  15.5 18.4 %all-to-all-start = ((bf16[128,8,512]{2,1,0:T(8,128)(2,1)}), bf16[128,8,512]{2,1,0:T(8,128)(2,1)S(1)}, u32[]{:S(2)}, u32[]{:S(2)}) async-start(bf16[128,8,512]{2,1,0:T(8,128)(2,1)} %bitcast_select_fusion), calls=%async_computation | async-start | bytes 2097152 | tf_op jit(solution)/shard_map/all_to_all | solution.py:40
  34.0 0.5 broadcast.165
  34.5 0.7 reduce.9
  35.2 0.7 reduce.11
  36.0 0.1 shift_right_arithmetic.27
  36.1 1.0 reduce.10
  37.1 5.6 %shift_right_arithmetic.23 = s32[128,64,4]{2,1,0:T(8,128)} reshape(s32[32768]{0:T(1024)S(1)} %reduce.10) | data formatting | bytes 262144 | tf_op jit(solution)/shard_map/shift_right_arithmetic | solution.py:13
  42.7 3.0 copy.20
  45.7 0.3 shift_right_arithmetic.24
  46.1 2.1 and_convert_fusion
  48.2 16.2 %all-to-all-done = bf16[128,8,512]{2,1,0:T(8,128)(2,1)S(1)} async-done(((bf16[128,8,512]{2,1,0:T(8,128)(2,1)}), bf16[128,8,512]{2,1,0:T(8,128)(2,1)S(1)}, u32[]{:S(2)}, u32[]{:S(2)}) %all-to-all-start) | async-done | bytes 1048608 | tf_op jit(solution)/shard_map/all_to_all | solution.py:40
  64.4 1.5 pad_maximum_fusion
  65.9 0.2 broadcast_in_dim.43
  66.1 58.5 %while.20 = (s32[]{:T(128)}, f32[16,64,512]{2,1,0:T(8,128)S(1)}, s32[4,32]{1,0:T(4,128)S(1)}, bf16[4,32,64,64]{2,3,1,0:T(8,128)(2,1)}, s32[4,32]{1,0:T(4,128)S(1)}, /*index=5*/bf16[32,64,512]{2,1,0:T(8,128)(2,1)}, s32[]{:T(128)}) while((s32[]{:T(128)}, f32[16,64,512]{2,1,0:T(8,128)S(1)}, s32[4,32]{1,0:T(4,128)S(1)}, ...), condition=%wide.region_2.3_spmd, body=%wide.region_0.0_spmd.sunk | while | flops 136316288 | bytes 23598240 | solution.py:57
  66.2 3.6 gather_fusion
  69.8 4.5 fusion.53
  74.3 6.5 %scatter_fusion = f32[16,64,512]{2,1,0:T(8,128)S(1)} fusion(f32[16,64,512]{2,1,0:T(8,128)S(1)} %get-tuple-element.210, s32[32]{0:T(128)S(1)} %get-tuple-element.192, f32[32,64,512]{2,1,0:T(8,128)} %fusion.53), kind=kCustom, calls=%fused_computation.3.clone.1 | custom fusion | flops 1048576 | bytes 12583040 | tf_op jit(solution)/shard_map/while/body/eval_jaxpr/scatter-add | solution.py:55
  80.8 3.6 gather_fusion
  84.4 4.5 fusion.53
  88.9 6.5 %scatter_fusion = f32[16,64,512]{2,1,0:T(8,128)S(1)} fusion(f32[16,64,512]{2,1,0:T(8,128)S(1)} %get-tuple-element.210, s32[32]{0:T(128)S(1)} %get-tuple-element.192, f32[32,64,512]{2,1,0:T(8,128)} %fusion.53), kind=kCustom, calls=%fused_computation.3.clone.1 | custom fusion | flops 1048576 | bytes 12583040 | tf_op jit(solution)/shard_map/while/body/eval_jaxpr/scatter-add | solution.py:55
  95.4 3.6 gather_fusion
  99.0 4.5 fusion.53
  103.5 6.5 %scatter_fusion = f32[16,64,512]{2,1,0:T(8,128)S(1)} fusion(f32[16,64,512]{2,1,0:T(8,128)S(1)} %get-tuple-element.210, s32[32]{0:T(128)S(1)} %get-tuple-element.192, f32[32,64,512]{2,1,0:T(8,128)} %fusion.53), kind=kCustom, calls=%fused_computation.3.clone.1 | custom fusion | flops 1048576 | bytes 12583040 | tf_op jit(solution)/shard_map/while/body/eval_jaxpr/scatter-add | solution.py:55
  110.1 3.6 gather_fusion
  113.7 4.5 fusion.53
  118.1 6.5 %scatter_fusion = f32[16,64,512]{2,1,0:T(8,128)S(1)} fusion(f32[16,64,512]{2,1,0:T(8,128)S(1)} %get-tuple-element.210, s32[32]{0:T(128)S(1)} %get-tuple-element.192, f32[32,64,512]{2,1,0:T(8,128)} %fusion.53), kind=kCustom, calls=%fused_computation.3.clone.1 | custom fusion | flops 1048576 | bytes 12583040 | tf_op jit(solution)/shard_map/while/body/eval_jaxpr/scatter-add | solution.py:55
  124.7 1.3 copy-done.1
  126.0 0.2 all-gather.5.cloned.1.call-start
  126.3 2.0 fusion.29
  128.3 80.2 %all-gather.3.cloned.1.call-done = f32[4,1024,512]{2,1,0:T(8,128)} async-done(((f32[1,1024,512]{2,1,0:T(8,128)}), f32[4,1024,512]{2,1,0:T(8,128)}) %all-gather.3.cloned.1.call-update) | async-done | bytes 8388624 | tf_op jit(solution)/shard_map/all_gather | solution.py:63
  208.6 4.6 reduce_sum.9
  213.2 3.0 multiply_convert_fusion
  216.2 1.0 fusion.24
  217.2 29.6 %all-gather.5.cloned.1.call-done = bf16[1024,512]{1,0:T(8,128)(2,1)} async-done(((bf16[256,512]{1,0:T(8,128)(2,1)}), bf16[1024,512]{1,0:T(8,128)(2,1)}) %all-gather.5.cloned.1.call-update) | async-done | bytes 1048592 | tf_op jit(solution)/shard_map/all_gather | solution.py:82
  246.8 2.5 broadcast_in_dim.46
  249.3 62.3 %while.21 = (s32[]{:T(128)}, f32[32,64,512]{2,1,0:T(8,128)}, s32[4,32]{1,0:T(4,128)S(1)}, bf16[4,32,64,64]{2,3,1,0:T(8,128)(2,1)}, s32[4,32]{1,0:T(4,128)S(1)}, /*index=5*/bf16[16,64,512]{2,1,0:T(8,128)(2,1)}, s32[]{:T(128)}) while((s32[]{:T(128)}, f32[32,64,512]{2,1,0:T(8,128)}, s32[4,32]{1,0:T(4,128)S(1)}, ...), condition=%wide.region_6.7_spmd, body=%wide.region_4.6_spmd.sunk | while | flops 136316288 | bytes 23598240 | solution.py:91
  249.3 1.9 gather_fusion.1
  251.2 3.7 fusion.57
  255.0 9.7 %scatter_fusion.1 = f32[32,64,512]{2,1,0:T(8,128)} fusion(f32[32,64,512]{2,1,0:T(8,128)} %get-tuple-element.231, s32[32]{0:T(128)S(1)} %get-tuple-element.200, f32[32,64,512]{2,1,0:T(8,128)} %fusion.57), kind=kCustom, calls=%fused_computation.4.clone.1 | custom fusion | flops 1048576 | bytes 12583040 | tf_op jit(solution)/shard_map/while/body/eval_jaxpr/scatter-add | solution.py:89
  264.8 1.9 gather_fusion.1
  266.7 3.7 fusion.57
  270.4 9.8 %scatter_fusion.1 = f32[32,64,512]{2,1,0:T(8,128)} fusion(f32[32,64,512]{2,1,0:T(8,128)} %get-tuple-element.231, s32[32]{0:T(128)S(1)} %get-tuple-element.200, f32[32,64,512]{2,1,0:T(8,128)} %fusion.57), kind=kCustom, calls=%fused_computation.4.clone.1 | custom fusion | flops 1048576 | bytes 12583040 | tf_op jit(solution)/shard_map/while/body/eval_jaxpr/scatter-add | solution.py:89
  280.3 1.9 gather_fusion.1
  282.2 3.7 fusion.57
  285.9 9.9 %scatter_fusion.1 = f32[32,64,512]{2,1,0:T(8,128)} fusion(f32[32,64,512]{2,1,0:T(8,128)} %get-tuple-element.231, s32[32]{0:T(128)S(1)} %get-tuple-element.200, f32[32,64,512]{2,1,0:T(8,128)} %fusion.57), kind=kCustom, calls=%fused_computation.4.clone.1 | custom fusion | flops 1048576 | bytes 12583040 | tf_op jit(solution)/shard_map/while/body/eval_jaxpr/scatter-add | solution.py:89
  295.9 1.9 gather_fusion.1
  297.8 3.7 fusion.57
  301.5 10.0 %scatter_fusion.1 = f32[32,64,512]{2,1,0:T(8,128)} fusion(f32[32,64,512]{2,1,0:T(8,128)} %get-tuple-element.231, s32[32]{0:T(128)S(1)} %get-tuple-element.200, f32[32,64,512]{2,1,0:T(8,128)} %fusion.57), kind=kCustom, calls=%fused_computation.4.clone.1 | custom fusion | flops 1048576 | bytes 12583040 | tf_op jit(solution)/shard_map/while/body/eval_jaxpr/scatter-add | solution.py:89
  311.6 2.7 slice.22
  314.3 15.9 %all-to-all-start.1 = ((bf16[128,8,512]{2,1,0:T(8,128)(2,1)}), bf16[128,8,512]{2,1,0:T(8,128)(2,1)}, u32[]{:S(2)}, u32[]{:S(2)}) async-start(bf16[128,8,512]{2,1,0:T(8,128)(2,1)} %bitcast.21), calls=%async_computation.1 | async-start | bytes 2097152 | tf_op jit(solution)/shard_map/all_to_all | solution.py:101
  330.3 1.9 slice.11
  332.1 28.2 %all-to-all-done.1 = bf16[128,8,512]{2,1,0:T(8,128)(2,1)} async-done(((bf16[128,8,512]{2,1,0:T(8,128)(2,1)}), bf16[128,8,512]{2,1,0:T(8,128)(2,1)}, u32[]{:S(2)}, u32[]{:S(2)}) %all-to-all-start.1) | async-done | bytes 1048608 | tf_op jit(solution)/shard_map/all_to_all | solution.py:101
  360.3 8.0 %scatter_custom_fusion.2 = f32[1024,512]{1,0:T(8,128)S(1)} fusion(f32[1024,512]{1,0:T(8,128)S(1)} %bitcast.83, s32[1024]{0:T(1024)S(1)} %bitcast.86, bf16[128,8,512]{2,1,0:T(8,128)(2,1)} %all-to-all-done.1), kind=kCustom, calls=%fused_computation.45 | custom fusion | flops 1048576 | bytes 3145728 | tf_op jit(solution)/shard_map/scatter-add | solution.py:105
  368.3 1.1 convert_element_type.58
  369.4 1.5 fusion.33
  370.9 1.3 fusion.27
  372.2 104.4 %all-reduce.2 = (bf16[512,512]{1,0:T(8,128)(2,1)}, bf16[512,512]{1,0:T(8,128)(2,1)}) all-reduce(f32[512,512]{1,0:T(8,128)S(1)} %fusion.27, f32[512,512]{1,0:T(8,128)S(1)} %fusion.33), channel_id=1, replica_groups=mesh['wide'=128,'rep'=4] {'wide','rep'}, use_global_device_ids=true, to_apply=%region_9.10 | all-reduce | flops 524288 | bytes 3145728 | tf_op jit(solution)/shard_map/psum | solution.py:80
  476.6 2.0 fusion.25
  (54 shorter events, 0.7 us)
Async XLA Ops:
  7.2 206.0 %copy-start = (bf16[512,512]{1,0:T(8,128)(2,1)S(1)}, bf16[512,512]{1,0:T(8,128)(2,1)}, u32[]{:S(2)}) copy-start(bf16[512,512]{1,0:T(8,128)(2,1)} %param.15) | copy-start | bytes 1572868
  14.3 20.2 %copy-start.7 = (s32[1,1,128]{2,1,0:T(1,128)S(1)}, s32[1,1,128]{2,1,0:T(1,128)}, u32[]{:S(2)}) copy-start(s32[1,1,128]{2,1,0:T(1,128)} %param.17) | copy-start | bytes 1540
  14.3 20.9 %copy-start.8 = (s32[1,1,128]{2,1,0:T(1,128)S(1)}, s32[1,1,128]{2,1,0:T(1,128)}, u32[]{:S(2)}) copy-start(s32[1,1,128]{2,1,0:T(1,128)} %param.18) | copy-start | bytes 1540
  14.4 21.8 %copy-start.5 = (s32[1,1,32768]{2,1,0:T(1,128)S(1)}, s32[1,1,32768]{2,1,0:T(1,128)}, u32[]{:S(2)}) copy-start(s32[1,1,32768]{2,1,0:T(1,128)} %param.19) | copy-start | bytes 393220
  15.5 48.9 %all-to-all-start = ((bf16[128,8,512]{2,1,0:T(8,128)(2,1)}), bf16[128,8,512]{2,1,0:T(8,128)(2,1)S(1)}, u32[]{:S(2)}, u32[]{:S(2)}) async-start(bf16[128,8,512]{2,1,0:T(8,128)(2,1)} %bitcast_select_fusion), calls=%async_computation | async-start | bytes 2097152 | tf_op jit(solution)/shard_map/all_to_all | solution.py:40
  34.0 174.6 %all-gather.3.cloned.1.call-start = ((), (), s32[]{:S(2)}) async-start(), calls=%async_computation.3 | async-start | bytes 10485760 | tf_op jit(solution)/shard_map/all_gather | solution.py:63
  46.1 18.3 %copy-start.2 = (bf16[1024,512]{1,0:T(8,128)(2,1)S(1)}, bf16[1024,512]{1,0:T(8,128)(2,1)}, u32[]{:S(2)}) copy-start(bf16[1024,512]{1,0:T(8,128)(2,1)} %param.13) | copy-start | bytes 3145732
  124.6 1.3 copy-start.1
  124.6 1.6 copy-start.6
  124.6 1.6 copy-start.4
  126.0 120.8 %all-gather.5.cloned.1.call-start = ((), (), s32[]{:S(2)}) async-start(), calls=%async_computation.4 | async-start | bytes 1310720 | tf_op jit(solution)/shard_map/all_gather | solution.py:82
  213.2 4.0 copy-start.3
  314.3 46.0 %all-to-all-start.1 = ((bf16[128,8,512]{2,1,0:T(8,128)(2,1)}), bf16[128,8,512]{2,1,0:T(8,128)(2,1)}, u32[]{:S(2)}, u32[]{:S(2)}) async-start(bf16[128,8,512]{2,1,0:T(8,128)(2,1)} %bitcast.21), calls=%async_computation.1 | async-start | bytes 2097152 | tf_op jit(solution)/shard_map/all_to_all | solution.py:101
  330.2 146.4 %reduce-scatter.2.cloned.1.call-start = ((), (), s32[]{:S(2)}) async-start(), calls=%async_computation.5 | async-start | bytes 1310720 | tf_op jit(solution)/shard_map/reduce_scatter | solution.py:107
Sparse Core Ops, SparseCore 0:
  126.1 82.4 all-gather.2
  217.4 29.3 all-gather.4
  369.5 20.3 reduce-scatter.1
